TPU v7x, 32 devices: a whole 2x2x4 slice. The times are simulated.
32 devices in a mesh: tm: 4 (over x, core), chan: 8 (over z, y).
Axes of the slice: x: 2, y: 2, z: 4, core: 2. Of those that a mesh axis runs over, the one named last changes fastest.
Arguments:
- samples: bfloat16 [384, 128], P('chan', 'tm'), may hold values from -6 to 6
- dead_channels: int32 [12], replicated, may hold values from 0 to 383
- first_kernel: bfloat16 [8, 32], replicated, may hold values from -3 to 3
- dilated_one: bfloat16 [3, 32, 64], replicated, may hold values from -0.875 to 0.875
- dilated_two: bfloat16 [3, 64, 128], replicated, may hold values from -0.625 to 0.625
- dilated_three: bfloat16 [3, 128, 256], replicated, may hold values from -0.4375 to 0.4375
- dilated_four: bfloat16 [3, 256, 256], replicated, may hold values from -0.3125 to 0.3125
- embed_weight: bfloat16 [256, 512], replicated, may hold values from -0.375 to 0.375
- gain_one: float32 [512], replicated, may hold values from 0.1 to 1.9
- project_in: bfloat16 [512, 1536], replicated, may hold values from -1 to 1
- project_out: bfloat16 [512, 512], replicated, may hold values from -0.25 to 0.25
- gain_two: float32 [512], replicated, may hold values from 0.1 to 1.9
- up_weight: bfloat16 [512, 2048], replicated, may hold values from -0.25 to 0.25
- down_weight: bfloat16 [2048, 512], replicated, may hold values from -0.125 to 0.125
Outputs:
- encoded: bfloat16 [32, 384, 512], P('tm', 'chan')
Inputs may be any that keep to these rules, and one draw needn't show every extreme that they name: `dead_channels`: channel numbers; a number may repeat.
All inputs are finite; a program needn't handle non-finite values.
Results may differ from a plain program's by a relative error of at most 0.015.
Values may be sent and summed in bfloat16 or wider, within the bound.
A program may use at most 64 MiB of HBM per device.

v0:
```python
import jax
import jax.numpy as jnp
from jax import lax
from jax.sharding import PartitionSpec as P

HEADS = 8
KERNEL = 8
STRIDE = 4
EPSILON = 1e-05
DILATIONS = (1, 2, 4, 8)


def extended_2(cells, sides, width):
    for axis, dim in sides:
        count = lax.axis_size(axis)
        ends = count - 1
        head = lax.slice_in_dim(cells, 0, width, axis=dim)
        tail = lax.slice_in_dim(cells, cells.shape[dim] - width, cells.shape[dim], axis=dim)
        cells = jnp.concatenate(
            [
                lax.ppermute(tail, axis, [(i, (i + 1) % count) for i in range(ends)]),
                cells,
                lax.ppermute(head, axis, [((i + 1) % count, i) for i in range(ends)]),
            ],
            axis=dim,
        )
    return cells


def normalize(tokens, gain):
    floats = tokens.astype(jnp.float32)
    average = jnp.mean(floats, axis=-1, keepdims=True)
    centred = floats - average
    variance = jnp.mean(centred * centred, axis=-1, keepdims=True)
    return (centred * lax.rsqrt(variance + EPSILON) * gain).astype(jnp.bfloat16)


def attend(query_rows, key_rows, value_rows, alive_mask):
    count = query_rows.shape[0]
    block_rows = min(512, count)
    scaling = query_rows.shape[2] ** (-0.5)

    def one_head(operands):
        queries, keys_head, values_head = operands
        blocks = queries.reshape(count // block_rows, block_rows, queries.shape[1])

        def one_block(query_block):
            scores = jnp.dot(query_block, keys_head.T, preferred_element_type=jnp.float32) * scaling
            scores = jnp.where(alive_mask[None, :], scores, -1e30)
            largest = jnp.max(scores, axis=1, keepdims=True)
            exponent = jnp.exp(scores - largest)
            weights = (exponent / jnp.sum(exponent, axis=1, keepdims=True)).astype(jnp.bfloat16)
            return jnp.dot(weights, values_head, preferred_element_type=jnp.float32).astype(
                jnp.bfloat16
            )

        return lax.map(one_block, blocks).reshape(count, queries.shape[1])

    heads_first = lax.map(
        one_head,
        (
            jnp.swapaxes(query_rows, 0, 1),
            jnp.swapaxes(key_rows, 0, 1),
            jnp.swapaxes(value_rows, 0, 1),
        ),
    )
    return jnp.swapaxes(heads_first, 0, 1).reshape(count, -1)


def encoder(
    embedded, alive_mask, gain_one, project_in, project_out, gain_two, up_weight, down_weight
):
    count, width = embedded.shape
    normed = normalize(embedded, gain_one)
    projected = jnp.dot(normed, project_in, preferred_element_type=jnp.float32).astype(jnp.bfloat16)
    pieces = projected.reshape(count, 3, HEADS, width // HEADS)
    attended = attend(pieces[:, 0], pieces[:, 1], pieces[:, 2], alive_mask)
    mixed = (
        embedded.astype(jnp.float32)
        + jnp.dot(attended, project_out, preferred_element_type=jnp.float32)
    ).astype(jnp.bfloat16)
    normed_two = normalize(mixed, gain_two)
    inner = jax.nn.gelu(jnp.dot(normed_two, up_weight, preferred_element_type=jnp.float32)).astype(
        jnp.bfloat16
    )
    return (
        mixed.astype(jnp.float32) + jnp.dot(inner, down_weight, preferred_element_type=jnp.float32)
    ).astype(jnp.bfloat16)


def patch_conv(padded, first_kernel, frames):
    taps = jnp.stack(
        [
            padded[:, offset : offset + STRIDE * (frames - 1) + 1 : STRIDE]
            for offset in range(KERNEL)
        ],
        axis=-1,
    )
    summed = jnp.einsum("cfk,ko->fco", taps, first_kernel, preferred_element_type=jnp.float32)
    return jax.nn.gelu(summed).astype(jnp.bfloat16)


def dilated(padded, weight, dilation, frames):
    summed = jnp.zeros((frames, padded.shape[1], weight.shape[2]), jnp.float32)
    for offset in range(3):
        window = padded[offset * dilation : offset * dilation + frames]
        summed = summed + jnp.einsum(
            "fci,io->fco", window, weight[offset], preferred_element_type=jnp.float32
        )
    return jax.nn.gelu(summed).astype(jnp.bfloat16)


def project_rows(features, embed_weight):
    return jnp.einsum(
        "fci,io->fco", features, embed_weight, preferred_element_type=jnp.float32
    ).astype(jnp.bfloat16)


def per_device(
    samples,
    dead_channels,
    first_kernel,
    dilated_one,
    dilated_two,
    dilated_three,
    dilated_four,
    embed_weight,
    gain_one,
    project_in,
    project_out,
    gain_two,
    up_weight,
    down_weight,
):
    channels_dev, sample_count = samples.shape
    groups = lax.axis_size("chan")
    channel_total = channels_dev * groups
    own_ids = lax.axis_index("chan") * channels_dev + jnp.arange(channels_dev, dtype=jnp.int32)
    own_alive = jnp.logical_not(jnp.any(own_ids[:, None] == dead_channels[None, :], axis=1))
    signal = jnp.where(own_alive[:, None], samples, jnp.zeros_like(samples))
    rim_width = (KERNEL - STRIDE) // 2
    weights_list = (dilated_one, dilated_two, dilated_three, dilated_four)
    padded = extended_2(signal, (("tm", 1),), rim_width)
    frames = sample_count // STRIDE
    hidden = patch_conv(padded, first_kernel, frames)
    for weight, dilation in zip(weights_list, DILATIONS):
        extended = extended_2(hidden, (("tm", 0),), dilation)
        hidden = dilated(extended, weight, dilation, frames)
    embedded = project_rows(hidden, embed_weight)
    embedded = lax.all_to_all(embedded, "chan", split_axis=0, concat_axis=1, tiled=True)
    all_ids = jnp.arange(channel_total, dtype=jnp.int32)
    alive_mask = jnp.logical_not(jnp.any(all_ids[:, None] == dead_channels[None, :], axis=1))

    def per_frame(frame_tokens):
        return encoder(
            frame_tokens,
            alive_mask,
            gain_one,
            project_in,
            project_out,
            gain_two,
            up_weight,
            down_weight,
        )

    result = lax.map(per_frame, embedded)
    return lax.all_to_all(result, "chan", split_axis=1, concat_axis=0, tiled=True)


def solution(mesh):
    return jax.shard_map(
        per_device,
        mesh=mesh,
        in_specs=(P("chan", "tm"), P(), P(), P(), P(), P(), P(), P(), P(), P(), P(), P(), P(), P()),
        out_specs=P("tm", "chan", None),
        check_vma=False,
    )
```

profile of v0, /device:TPU:0, one launch (start us, length us, event | category | flops | bytes accessed | tf_op | source)
XLA Modules:
  0.0 116.4 jit_solution(12862702731849805293)
XLA Ops:
  1.6 2.4 %collective-permute-start = (bf16[48,2]{0,1:T(2,128)(2,1)S(1)}, bf16[48,2]{0,1:T(2,128)(2,1)S(1)}, u32[]{:S(2)}, u32[]{:S(2)}) collective-permute-start(bf16[48,2]{0,1:T(2,128)(2,1)S(1)} %get-tuple-element.175), channel_id=1, source_target_pairs={{0,8},{8,16},{16,24},{1,9},{9,17},{17,25},{2,10},{10,18},{18,26},{... | collective-permute-start | bytes 584 | tf_op jit(solution)/shard_map/ppermute | solution.py:21
  5.5 3.7 %collective-permute-done.1 = bf16[48,2]{0,1:T(2,128)(2,1)S(1)} collective-permute-done((bf16[48,2]{0,1:T(2,128)(2,1)S(1)}, bf16[48,2]{0,1:T(2,128)(2,1)S(1)}, u32[]{:S(2)}, u32[]{:S(2)}) %collective-permute-start.1) | collective-permute-done | bytes 224 | tf_op jit(solution)/shard_map/ppermute | solution.py:23
  11.6 4.9 %collective-permute-start.2 = (bf16[1,48,32]{1,2,0:T(8,128)(2,1)S(1)}, bf16[1,48,32]{1,2,0:T(8,128)(2,1)S(1)}, u32[]{:S(2)}, u32[]{:S(2)}) collective-permute-start(bf16[1,48,32]{1,2,0:T(8,128)(2,1)S(1)} %get-tuple-element.173), channel_id=1, source_target_pairs={{0,8},{8,16},{16,24},{1,9},{9,17},{17,25},{2,10},{10,18},{18,26},{... | collective-permute-start | bytes 9224 | tf_op jit(solution)/shard_map/ppermute | solution.py:21
  21.6 4.3 %collective-permute-start.4 = (bf16[2,48,64]{2,1,0:T(8,128)(2,1)S(1)}, bf16[2,48,64]{2,1,0:T(8,128)(2,1)S(1)}, u32[]{:S(2)}, u32[]{:S(2)}) collective-permute-start(bf16[2,48,64]{2,1,0:T(8,128)(2,1)S(1)} %get-tuple-element.171), channel_id=1, source_target_pairs={{0,8},{8,16},{16,24},{1,9},{9,17},{17,25},{2,10},{10,18},{18,26},{... | collective-permute-start | bytes 36872 | tf_op jit(solution)/shard_map/ppermute | solution.py:21
  28.6 4.4 %collective-permute-start.6 = (bf16[4,48,128]{2,1,0:T(8,128)(2,1)S(1)}, bf16[4,48,128]{2,1,0:T(8,128)(2,1)S(1)}, u32[]{:S(2)}, u32[]{:S(2)}) collective-permute-start(bf16[4,48,128]{2,1,0:T(8,128)(2,1)S(1)} %get-tuple-element.169), channel_id=1, source_target_pairs={{0,8},{8,16},{16,24},{1,9},{9,17},{17,25},{2,10},{10,18},{18,26},{... | collective-permute-start | bytes 147464 | tf_op jit(solution)/shard_map/ppermute | solution.py:21
  35.5 5.8 %collective-permute-start.8 = (bf16[8,48,256]{2,1,0:T(8,128)(2,1)S(1)}, bf16[8,48,256]{2,1,0:T(8,128)(2,1)}, u32[]{:S(2)}, u32[]{:S(2)}) collective-permute-start(bf16[8,48,256]{2,1,0:T(8,128)(2,1)S(1)} %fusion.47), channel_id=1, source_target_pairs={{0,8},{8,16},{16,24},{1,9},{9,17},{17,25},{2,10},{10,18},{18,26},{... | collective-permute-start | bytes 589832 | tf_op jit(solution)/shard_map/ppermute | solution.py:21
  41.8 2.1 %convolution_convert_fusion.2 = bf16[8,48,512]{2,1,0:T(8,128)(2,1)} fusion(f32[8,48,256]{2,1,0:T(8,128)S(1)} %fusion.99, f32[8,48,256]{2,1,0:T(8,128)S(1)} %fusion.101, bf16[8,48,256]{2,1,0:T(8,128)(2,1)} %collective-permute-done.8, bf16[256,512]{1,0:T(8,128)(2,1)S(1)} %copy-done.5, bf16[3,256,256]{2,1,0:T(8,128)(2,1)S(1)} %copy-done.1), kind=kOutput, calls=%fused_computation.32 | convolution fusion | flops 152272896 | bytes 1769472 | tf_op jit(solution)/shard_map/fci,io->fco/dot_general | solution.py:114
  43.9 5.8 %all-to-all-start = ((bf16[8,48,512]{2,1,0:T(8,128)(2,1)}), bf16[8,48,512]{2,1,0:T(8,128)(2,1)S(1)}, u32[]{:S(2)}, u32[]{:S(2)}) async-start(bf16[8,48,512]{2,1,0:T(8,128)(2,1)} %convolution_convert_fusion.2), calls=%async_computation | async-start | bytes 786432 | tf_op jit(solution)/shard_map/all_to_all | solution.py:150
  49.9 9.2 %all-to-all-done = bf16[8,48,512]{2,1,0:T(8,128)(2,1)S(1)} async-done(((bf16[8,48,512]{2,1,0:T(8,128)(2,1)}), bf16[8,48,512]{2,1,0:T(8,128)(2,1)S(1)}, u32[]{:S(2)}, u32[]{:S(2)}) %all-to-all-start) | async-done | bytes 393248 | tf_op jit(solution)/shard_map/all_to_all | solution.py:150
  59.8 3.2 %convolution_convert_fusion.1 = bf16[384,1536]{1,0:T(8,128)(2,1)} fusion(bf16[384,512]{1,0:T(8,128)(2,1)S(1)} %fusion.39, bf16[512,1536]{1,0:T(8,128)(2,1)} %param.25), kind=kOutput, calls=%fused_computation.25 | convolution fusion | flops 604569600 | bytes 3145728 | tf_op jit(solution)/shard_map/while/body/eval_jaxpr/dot_general | solution.py:75
  63.1 2.4 %copy.148 = bf16[384,1536]{0,1:T(8,128)(2,1)} copy(bf16[384,1536]{1,0:T(8,128)(2,1)} %convolution_convert_fusion.1) | data formatting | bytes 2359296 | tf_op jit(solution)/shard_map/while/body/eval_jaxpr/convert_element_type | solution.py:75
  65.4 2.1 %slice_bitcast_fusion = (bf16[8,384,64]{1,2,0:T(8,128)(2,1)}, bf16[8,384,64]{1,2,0:T(8,128)(2,1)S(1)}, bf16[8,384,64]{1,2,0:T(8,128)(2,1)S(1)}) fusion(bf16[384,3,8,64]{0,3,2,1:T(8,128)(2,1)} %bitcast.143), kind=kLoop, calls=%fused_computation.70 | loop fusion | bytes 2359296 | tf_op jit(solution)/shard_map/while/body/eval_jaxpr/transpose | solution.py:64
  67.6 16.7 %while.17 = (s32[]{:T(128)}, bf16[8,384,64]{1,2,0:T(8,128)(2,1)}, pred[384]{0:T(512)(128)(4,1)S(1)}, bf16[8,384,64]{1,2,0:T(8,128)(2,1)S(1)}, bf16[8,384,64]{1,2...) while((s32[]{:T(128)}, bf16[8,384,64]{1,2,0:T(8,128)(2,1)}, pred[384]{0:T(512)(128)(4,1)S(1)}, ...), condition=%wide.region_7.8_spmd, body=%wide.region_4.7_spmd.sunk | while | flops 38952192 | bytes 1976397 | solution.py:59
  68.0 1.7 %fusion.186 = bf16[8,384,64]{1,2,0:T(8,128)(2,1)} fusion(bf16[8,384,64]{1,2,0:T(8,128)(2,1)} %get-tuple-element.228, s32[]{:T(128)} %get-tuple-element.227, f32[384,384]{0,1:T(8,128)S(1)} %get-tuple-element.218, f32[384]{0:T(512)S(1)} %fusion.185, f32[384]{0:T(512)S(1)} %get-tuple-element.219, bf16[8,384,64]{1,2,0:T(8,128)(2,1)} %get-tuple-element.239), kind=kOutput, calls=%fused_computation.4.clone.1 | convolution fusion | flops 19341312 | bytes 692224 | tf_op jit(solution)/shard_map/while/body/eval_jaxpr/while/body/eval_jaxpr/while/body/eval_jaxpr/dot_general | solution.py:53
  70.1 1.7 %fusion.186 = bf16[8,384,64]{1,2,0:T(8,128)(2,1)} fusion(bf16[8,384,64]{1,2,0:T(8,128)(2,1)} %get-tuple-element.228, s32[]{:T(128)} %get-tuple-element.227, f32[384,384]{0,1:T(8,128)S(1)} %get-tuple-element.218, f32[384]{0:T(512)S(1)} %fusion.185, f32[384]{0:T(512)S(1)} %get-tuple-element.219, bf16[8,384,64]{1,2,0:T(8,128)(2,1)} %get-tuple-element.239), kind=kOutput, calls=%fused_computation.4.clone.1 | convolution fusion | flops 19341312 | bytes 692224 | tf_op jit(solution)/shard_map/while/body/eval_jaxpr/while/body/eval_jaxpr/while/body/eval_jaxpr/dot_general | solution.py:53
  72.2 1.7 %fusion.186 = bf16[8,384,64]{1,2,0:T(8,128)(2,1)} fusion(bf16[8,384,64]{1,2,0:T(8,128)(2,1)} %get-tuple-element.228, s32[]{:T(128)} %get-tuple-element.227, f32[384,384]{0,1:T(8,128)S(1)} %get-tuple-element.218, f32[384]{0:T(512)S(1)} %fusion.185, f32[384]{0:T(512)S(1)} %get-tuple-element.219, bf16[8,384,64]{1,2,0:T(8,128)(2,1)} %get-tuple-element.239), kind=kOutput, calls=%fused_computation.4.clone.1 | convolution fusion | flops 19341312 | bytes 692224 | tf_op jit(solution)/shard_map/while/body/eval_jaxpr/while/body/eval_jaxpr/while/body/eval_jaxpr/dot_general | solution.py:53
  74.3 1.7 %fusion.186 = bf16[8,384,64]{1,2,0:T(8,128)(2,1)} fusion(bf16[8,384,64]{1,2,0:T(8,128)(2,1)} %get-tuple-element.228, s32[]{:T(128)} %get-tuple-element.227, f32[384,384]{0,1:T(8,128)S(1)} %get-tuple-element.218, f32[384]{0:T(512)S(1)} %fusion.185, f32[384]{0:T(512)S(1)} %get-tuple-element.219, bf16[8,384,64]{1,2,0:T(8,128)(2,1)} %get-tuple-element.239), kind=kOutput, calls=%fused_computation.4.clone.1 | convolution fusion | flops 19341312 | bytes 692224 | tf_op jit(solution)/shard_map/while/body/eval_jaxpr/while/body/eval_jaxpr/while/body/eval_jaxpr/dot_general | solution.py:53
  76.3 1.7 %fusion.186 = bf16[8,384,64]{1,2,0:T(8,128)(2,1)} fusion(bf16[8,384,64]{1,2,0:T(8,128)(2,1)} %get-tuple-element.228, s32[]{:T(128)} %get-tuple-element.227, f32[384,384]{0,1:T(8,128)S(1)} %get-tuple-element.218, f32[384]{0:T(512)S(1)} %fusion.185, f32[384]{0:T(512)S(1)} %get-tuple-element.219, bf16[8,384,64]{1,2,0:T(8,128)(2,1)} %get-tuple-element.239), kind=kOutput, calls=%fused_computation.4.clone.1 | convolution fusion | flops 19341312 | bytes 692224 | tf_op jit(solution)/shard_map/while/body/eval_jaxpr/while/body/eval_jaxpr/while/body/eval_jaxpr/dot_general | solution.py:53
  78.4 1.7 %fusion.186 = bf16[8,384,64]{1,2,0:T(8,128)(2,1)} fusion(bf16[8,384,64]{1,2,0:T(8,128)(2,1)} %get-tuple-element.228, s32[]{:T(128)} %get-tuple-element.227, f32[384,384]{0,1:T(8,128)S(1)} %get-tuple-element.218, f32[384]{0:T(512)S(1)} %fusion.185, f32[384]{0:T(512)S(1)} %get-tuple-element.219, bf16[8,384,64]{1,2,0:T(8,128)(2,1)} %get-tuple-element.239), kind=kOutput, calls=%fused_computation.4.clone.1 | convolution fusion | flops 19341312 | bytes 692224 | tf_op jit(solution)/shard_map/while/body/eval_jaxpr/while/body/eval_jaxpr/while/body/eval_jaxpr/dot_general | solution.py:53
  80.5 1.7 %fusion.186 = bf16[8,384,64]{1,2,0:T(8,128)(2,1)} fusion(bf16[8,384,64]{1,2,0:T(8,128)(2,1)} %get-tuple-element.228, s32[]{:T(128)} %get-tuple-element.227, f32[384,384]{0,1:T(8,128)S(1)} %get-tuple-element.218, f32[384]{0:T(512)S(1)} %fusion.185, f32[384]{0:T(512)S(1)} %get-tuple-element.219, bf16[8,384,64]{1,2,0:T(8,128)(2,1)} %get-tuple-element.239), kind=kOutput, calls=%fused_computation.4.clone.1 | convolution fusion | flops 19341312 | bytes 692224 | tf_op jit(solution)/shard_map/while/body/eval_jaxpr/while/body/eval_jaxpr/while/body/eval_jaxpr/dot_general | solution.py:53
  82.6 1.7 %fusion.186 = bf16[8,384,64]{1,2,0:T(8,128)(2,1)} fusion(bf16[8,384,64]{1,2,0:T(8,128)(2,1)} %get-tuple-element.228, s32[]{:T(128)} %get-tuple-element.227, f32[384,384]{0,1:T(8,128)S(1)} %get-tuple-element.218, f32[384]{0:T(512)S(1)} %fusion.185, f32[384]{0:T(512)S(1)} %get-tuple-element.219, bf16[8,384,64]{1,2,0:T(8,128)(2,1)} %get-tuple-element.239), kind=kOutput, calls=%fused_computation.4.clone.1 | convolution fusion | flops 19341312 | bytes 692224 | tf_op jit(solution)/shard_map/while/body/eval_jaxpr/while/body/eval_jaxpr/while/body/eval_jaxpr/dot_general | solution.py:53
  86.2 4.4 %fusion.30 = bf16[1,384,512]{2,1,0:T(8,128)(2,1)} fusion(f32[384,512]{1,0:T(8,128)S(1)} %get-tuple-element.178, bf16[2048,512]{1,0:T(8,128)(2,1)S(1)} %copy-done, bf16[512,2048]{1,0:T(8,128)(2,1)} %param.28, f32[512]{0:T(512)S(1)} %copy-done.6, f32[384]{0:T(512)S(1)} %add_rsqrt_fusion.1, f32[384]{0:T(512)S(1)} %broadcast_multiply_fusion.1), kind=kOutput, calls=%fused_computation.33 | convolution fusion | flops 1618870272 | bytes 5379072 | tf_op jit(solution)/shard_map/while/body/eval_jaxpr/dot_general | solution.py:87
  92.7 3.0 %reduce.8 = bf16[384,512]{1,0:T(8,128)(2,1)S(1)} reduce(bf16[384,1,512]{2,1,0:T(2,128)(2,1)S(1)} %bitcast.144, bf16[]{:T(256)} %broadcast.175), dimensions={1}, to_apply=%bitcast.133.reduce_sub_computation | reduce | bytes 786434
  96.0 19.2 %all_to_all.21 = bf16[8,2,12288]{2,1,0:T(2,128)(2,1)S(1)} all-to-all(bf16[8,2,12288]{2,1,0:T(2,128)(2,1)S(1)} %reshape.104), channel_id=1, replica_groups=mesh['tm'=4,'chan'=8] {'chan'}, dimensions={0} | all-to-all | bytes 786432 | tf_op jit(solution)/shard_map/all_to_all | solution.py:167
  (103 shorter events, 25.9 us)
Async XLA Ops:
  0.0 86.2 %copy-start = (bf16[2048,512]{1,0:T(8,128)(2,1)S(1)}, bf16[2048,512]{1,0:T(8,128)(2,1)}, u32[]{:S(2)}) copy-start(bf16[2048,512]{1,0:T(8,128)(2,1)} %param.29) | copy-start | bytes 6291460
  0.0 25.9 %copy-start.3 = (bf16[3,64,128]{2,1,0:T(8,128)(2,1)S(1)}, bf16[3,64,128]{2,1,0:T(8,128)(2,1)}, u32[]{:S(2)}) copy-start(bf16[3,64,128]{2,1,0:T(8,128)(2,1)} %param.20) | copy-start | bytes 147460
  0.0 28.4 %copy-start.2 = (bf16[3,128,256]{2,1,0:T(8,128)(2,1)S(1)}, bf16[3,128,256]{2,1,0:T(8,128)(2,1)}, u32[]{:S(2)}) copy-start(bf16[3,128,256]{2,1,0:T(8,128)(2,1)} %param.21) | copy-start | bytes 589828
  1.6 3.8 %collective-permute-start = (bf16[48,2]{0,1:T(2,128)(2,1)S(1)}, bf16[48,2]{0,1:T(2,128)(2,1)S(1)}, u32[]{:S(2)}, u32[]{:S(2)}) collective-permute-start(bf16[48,2]{0,1:T(2,128)(2,1)S(1)} %get-tuple-element.175), channel_id=1, source_target_pairs={{0,8},{8,16},{16,24},{1,9},{9,17},{17,25},{2,10},{10,18},{18,26},{... | collective-permute-start | bytes 584 | tf_op jit(solution)/shard_map/ppermute | solution.py:21
  4.0 5.1 %collective-permute-start.1 = (bf16[48,2]{0,1:T(2,128)(2,1)S(1)}, bf16[48,2]{0,1:T(2,128)(2,1)S(1)}, u32[]{:S(2)}, u32[]{:S(2)}) collective-permute-start(bf16[48,2]{0,1:T(2,128)(2,1)S(1)} %get-tuple-element.176), channel_id=1, source_target_pairs={{8,0},{16,8},{24,16},{9,1},{17,9},{25,17},{10,2},{18,10},{26,18},{... | collective-permute-start | bytes 584 | tf_op jit(solution)/shard_map/ppermute | solution.py:23
  10.3 7.1 %collective-permute-start.3 = (bf16[1,48,32]{1,2,0:T(8,128)(2,1)S(1)}, bf16[1,48,32]{1,2,0:T(8,128)(2,1)S(1)}, u32[]{:S(2)}, u32[]{:S(2)}) collective-permute-start(bf16[1,48,32]{1,2,0:T(8,128)(2,1)S(1)} %get-tuple-element.174), channel_id=1, source_target_pairs={{8,0},{16,8},{24,16},{9,1},{17,9},{25,17},{10,2},{18,10},{26,18},{... | collective-permute-start | bytes 9224 | tf_op jit(solution)/shard_map/ppermute | solution.py:23
  11.6 6.7 %collective-permute-start.2 = (bf16[1,48,32]{1,2,0:T(8,128)(2,1)S(1)}, bf16[1,48,32]{1,2,0:T(8,128)(2,1)S(1)}, u32[]{:S(2)}, u32[]{:S(2)}) collective-permute-start(bf16[1,48,32]{1,2,0:T(8,128)(2,1)S(1)} %get-tuple-element.173), channel_id=1, source_target_pairs={{0,8},{8,16},{16,24},{1,9},{9,17},{17,25},{2,10},{10,18},{18,26},{... | collective-permute-start | bytes 9224 | tf_op jit(solution)/shard_map/ppermute | solution.py:21
  19.3 22.0 %copy-start.1 = (bf16[3,256,256]{2,1,0:T(8,128)(2,1)S(1)}, bf16[3,256,256]{2,1,0:T(8,128)(2,1)}, u32[]{:S(2)}) copy-start(bf16[3,256,256]{2,1,0:T(8,128)(2,1)} %param.22) | copy-start | bytes 1179652
  19.3 6.6 %collective-permute-start.5 = (bf16[2,48,64]{2,1,0:T(8,128)(2,1)S(1)}, bf16[2,48,64]{2,1,0:T(8,128)(2,1)S(1)}, u32[]{:S(2)}, u32[]{:S(2)}) collective-permute-start(bf16[2,48,64]{2,1,0:T(8,128)(2,1)S(1)} %get-tuple-element.172), channel_id=1, source_target_pairs={{8,0},{16,8},{24,16},{9,1},{17,9},{25,17},{10,2},{18,10},{26,18},{... | collective-permute-start | bytes 36872 | tf_op jit(solution)/shard_map/ppermute | solution.py:23
  21.6 5.1 %collective-permute-start.4 = (bf16[2,48,64]{2,1,0:T(8,128)(2,1)S(1)}, bf16[2,48,64]{2,1,0:T(8,128)(2,1)S(1)}, u32[]{:S(2)}, u32[]{:S(2)}) collective-permute-start(bf16[2,48,64]{2,1,0:T(8,128)(2,1)S(1)} %get-tuple-element.171), channel_id=1, source_target_pairs={{0,8},{8,16},{16,24},{1,9},{9,17},{17,25},{2,10},{10,18},{18,26},{... | collective-permute-start | bytes 36872 | tf_op jit(solution)/shard_map/ppermute | solution.py:21
  26.9 14.9 %copy-start.5 = (bf16[256,512]{1,0:T(8,128)(2,1)S(1)}, bf16[256,512]{1,0:T(8,128)(2,1)}, u32[]{:S(2)}) copy-start(bf16[256,512]{1,0:T(8,128)(2,1)} %param.23) | copy-start | bytes 786436
  27.0 6.0 %collective-permute-start.7 = (bf16[4,48,128]{2,1,0:T(8,128)(2,1)S(1)}, bf16[4,48,128]{2,1,0:T(8,128)(2,1)S(1)}, u32[]{:S(2)}, u32[]{:S(2)}) collective-permute-start(bf16[4,48,128]{2,1,0:T(8,128)(2,1)S(1)} %get-tuple-element.170), channel_id=1, source_target_pairs={{8,0},{16,8},{24,16},{9,1},{17,9},{25,17},{10,2},{18,10},{26,18},{... | collective-permute-start | bytes 147464 | tf_op jit(solution)/shard_map/ppermute | solution.py:23
  28.6 5.2 %collective-permute-start.6 = (bf16[4,48,128]{2,1,0:T(8,128)(2,1)S(1)}, bf16[4,48,128]{2,1,0:T(8,128)(2,1)S(1)}, u32[]{:S(2)}, u32[]{:S(2)}) collective-permute-start(bf16[4,48,128]{2,1,0:T(8,128)(2,1)S(1)} %get-tuple-element.169), channel_id=1, source_target_pairs={{0,8},{8,16},{16,24},{1,9},{9,17},{17,25},{2,10},{10,18},{18,26},{... | collective-permute-start | bytes 147464 | tf_op jit(solution)/shard_map/ppermute | solution.py:21
  34.1 15.6 %copy-start.7 = (s32[12]{0:T(128)S(1)}, s32[12]{0:T(128)}, u32[]{:S(2)}) copy-start(s32[12]{0:T(128)} %param.17) | copy-start | bytes 148
  34.2 7.3 %collective-permute-start.9 = (bf16[8,48,256]{2,1,0:T(8,128)(2,1)S(1)}, bf16[8,48,256]{2,1,0:T(8,128)(2,1)S(1)}, u32[]{:S(2)}, u32[]{:S(2)}) collective-permute-start(bf16[8,48,256]{2,1,0:T(8,128)(2,1)S(1)} %fusion.47), channel_id=1, source_target_pairs={{8,0},{16,8},{24,16},{9,1},{17,9},{25,17},{10,2},{18,10},{26,18},{... | collective-permute-start | bytes 589832 | tf_op jit(solution)/shard_map/ppermute | solution.py:23
  35.5 6.3 %collective-permute-start.8 = (bf16[8,48,256]{2,1,0:T(8,128)(2,1)S(1)}, bf16[8,48,256]{2,1,0:T(8,128)(2,1)}, u32[]{:S(2)}, u32[]{:S(2)}) collective-permute-start(bf16[8,48,256]{2,1,0:T(8,128)(2,1)S(1)} %fusion.47), channel_id=1, source_target_pairs={{0,8},{8,16},{16,24},{1,9},{9,17},{17,25},{2,10},{10,18},{18,26},{... | collective-permute-start | bytes 589832 | tf_op jit(solution)/shard_map/ppermute | solution.py:21
  41.5 18.1 %copy-start.4 = (f32[512]{0:T(512)S(1)}, f32[512]{0:T(512)}, u32[]{:S(2)}) copy-start(f32[512]{0:T(512)} %param.24) | copy-start | bytes 6148
  43.9 15.1 %all-to-all-start = ((bf16[8,48,512]{2,1,0:T(8,128)(2,1)}), bf16[8,48,512]{2,1,0:T(8,128)(2,1)S(1)}, u32[]{:S(2)}, u32[]{:S(2)}) async-start(bf16[8,48,512]{2,1,0:T(8,128)(2,1)} %convolution_convert_fusion.2), calls=%async_computation | async-start | bytes 786432 | tf_op jit(solution)/shard_map/all_to_all | solution.py:150
  84.3 1.9 %copy-start.6 = (f32[512]{0:T(512)S(1)}, f32[512]{0:T(512)}, u32[]{:S(2)}) copy-start(f32[512]{0:T(512)} %param.27) | copy-start | bytes 6148
where the time goes:
time: 118 us; the launch traced here: 116 us
  starting transfers between devices  34.3 us (29%)
  matrix products  33.1 us (28%)
  blocking collectives  19.2 us (16%)
  waiting for transfers between devices  14.2 us (12%)
  local copies, waits for them, and re-layouts  8.62 us (7%)
  other arithmetic  6.6 us (6%)
    ppermute x5, starting transfers between devices, extended_2(): lax.ppermute(tail, axis, [(i, (i + 1) % count) for i in range(ends)])  21.7 us
    all_to_all x1, blocking collectives, per_device(): lax.all_to_all(result, 'chan', split_axis=1, concat_axis=0, tiled=True)  19.2 us
    dot_general x8, matrix products, one_block(): jnp.dot(weights, values_head, preferred_element_type=jnp.float32)  13.3 us
    all_to_all x1, waiting for transfers between devices, per_device(): lax.all_to_all(embedded, 'chan', split_axis=0, concat_axis=1, tiled=True)  9.17 us
    ppermute x5, starting transfers between devices, extended_2(): lax.ppermute(head, axis, [((i + 1) % count, i) for i in range(ends)])  6.72 us
    all_to_all x1, starting transfers between devices, per_device(): lax.all_to_all(embedded, 'chan', split_axis=0, concat_axis=1, tiled=True)  5.83 us
    dot_general x11, matrix products, dilated(): jnp.einsum('fci,io->fco', window, weight[offset], preferred_element_type=...  5.04 us
    dot_general x1, matrix products, encoder(): jnp.dot(inner, down_weight, preferred_element_type=jnp.float32)  4.41 us
  transfers between devices with their start and end apart: 11, of which 5 were waited for; matrix products, arithmetic and copies ran while one was open for 3% of the time, Pallas kernels for 0%

commit v1 on v0

--- a/solution.py
+++ b/solution.py
@@ -147,7 +147,10 @@
         extended = extended_2(hidden, (("tm", 0),), dilation)
         hidden = dilated(extended, weight, dilation, frames)
     embedded = project_rows(hidden, embed_weight)
-    embedded = lax.all_to_all(embedded, "chan", split_axis=0, concat_axis=1, tiled=True)
+    embedded = jnp.concatenate(
+        lax.all_to_all(jnp.stack(jnp.split(embedded, lax.axis_size("chan"), axis=0)), "chan", 0, 0),
+        axis=1,
+    )
     all_ids = jnp.arange(channel_total, dtype=jnp.int32)
     alive_mask = jnp.logical_not(jnp.any(all_ids[:, None] == dead_channels[None, :], axis=1))
 

time: 118 us -> 122 us (1.034)
  local copies, waits for them, and re-layouts: 8.62 us -> 13.6 us
    unnamed x20 -> x27, local copies, waits for them, and re-layouts: 2.01 us -> 6.33 us
where the time goes in v1:
time: 122 us; the launch traced here: 121 us
  starting transfers between devices  34.2 us (28%)
  matrix products  32.4 us (27%)
  blocking collectives  19.2 us (16%)
  waiting for transfers between devices  14.2 us (12%)
  local copies, waits for them, and re-layouts  13.6 us (11%)
  other arithmetic  6.6 us (5%)
    ppermute x5, starting transfers between devices, extended_2(): lax.ppermute(tail, axis, [(i, (i + 1) % count) for i in range(ends)])  21.7 us
    all_to_all x1, blocking collectives, per_device(): lax.all_to_all(result, 'chan', split_axis=1, concat_axis=0, tiled=True)  19.2 us
    dot_general x8, matrix products, one_block(): jnp.dot(weights, values_head, preferred_element_type=jnp.float32)  13.3 us
    all_to_all x1, waiting for transfers between devices, per_device(): lax.all_to_all(jnp.stack(jnp.split(embedded, lax.axis_size('chan'), axis=...  9.17 us
    ppermute x5, starting transfers between devices, extended_2(): lax.ppermute(head, axis, [((i + 1) % count, i) for i in range(ends)])  6.72 us
    unnamed x27, local copies, waits for them, and re-layouts  6.33 us
    all_to_all x1, starting transfers between devices, per_device(): lax.all_to_all(jnp.stack(jnp.split(embedded, lax.axis_size('chan'), axis=...  5.83 us
    dot_general x11, matrix products, dilated(): jnp.einsum('fci,io->fco', window, weight[offset], preferred_element_type=...  5.04 us
  transfers between devices with their start and end apart: 11, of which 5 were waited for; matrix products, arithmetic and copies ran while one was open for 3% of the time, Pallas kernels for 0%

profile of v1, /device:TPU:0, one launch (start us, length us, event | category | flops | bytes accessed | tf_op | source)
XLA Modules:
  0.0 120.7 jit_solution(15530693608249716825)
XLA Ops:
  1.6 2.4 %collective-permute-start = (bf16[48,2]{0,1:T(2,128)(2,1)S(1)}, bf16[48,2]{0,1:T(2,128)(2,1)S(1)}, u32[]{:S(2)}, u32[]{:S(2)}) collective-permute-start(bf16[48,2]{0,1:T(2,128)(2,1)S(1)} %get-tuple-element.175), channel_id=1, source_target_pairs={{0,8},{8,16},{16,24},{1,9},{9,17},{17,25},{2,10},{10,18},{18,26},{... | collective-permute-start | bytes 584 | tf_op jit(solution)/shard_map/ppermute | solution.py:21
  5.5 3.7 %collective-permute-done.1 = bf16[48,2]{0,1:T(2,128)(2,1)S(1)} collective-permute-done((bf16[48,2]{0,1:T(2,128)(2,1)S(1)}, bf16[48,2]{0,1:T(2,128)(2,1)S(1)}, u32[]{:S(2)}, u32[]{:S(2)}) %collective-permute-start.1) | collective-permute-done | bytes 224 | tf_op jit(solution)/shard_map/ppermute | solution.py:23
  11.6 4.9 %collective-permute-start.2 = (bf16[1,48,32]{1,2,0:T(8,128)(2,1)S(1)}, bf16[1,48,32]{1,2,0:T(8,128)(2,1)S(1)}, u32[]{:S(2)}, u32[]{:S(2)}) collective-permute-start(bf16[1,48,32]{1,2,0:T(8,128)(2,1)S(1)} %get-tuple-element.173), channel_id=1, source_target_pairs={{0,8},{8,16},{16,24},{1,9},{9,17},{17,25},{2,10},{10,18},{18,26},{... | collective-permute-start | bytes 9224 | tf_op jit(solution)/shard_map/ppermute | solution.py:21
  21.6 4.3 %collective-permute-start.4 = (bf16[2,48,64]{2,1,0:T(8,128)(2,1)S(1)}, bf16[2,48,64]{2,1,0:T(8,128)(2,1)S(1)}, u32[]{:S(2)}, u32[]{:S(2)}) collective-permute-start(bf16[2,48,64]{2,1,0:T(8,128)(2,1)S(1)} %get-tuple-element.171), channel_id=1, source_target_pairs={{0,8},{8,16},{16,24},{1,9},{9,17},{17,25},{2,10},{10,18},{18,26},{... | collective-permute-start | bytes 36872 | tf_op jit(solution)/shard_map/ppermute | solution.py:21
  28.6 4.4 %collective-permute-start.6 = (bf16[4,48,128]{2,1,0:T(8,128)(2,1)S(1)}, bf16[4,48,128]{2,1,0:T(8,128)(2,1)S(1)}, u32[]{:S(2)}, u32[]{:S(2)}) collective-permute-start(bf16[4,48,128]{2,1,0:T(8,128)(2,1)S(1)} %get-tuple-element.169), channel_id=1, source_target_pairs={{0,8},{8,16},{16,24},{1,9},{9,17},{17,25},{2,10},{10,18},{18,26},{... | collective-permute-start | bytes 147464 | tf_op jit(solution)/shard_map/ppermute | solution.py:21
  35.4 5.8 %collective-permute-start.8 = (bf16[8,48,256]{2,1,0:T(8,128)(2,1)S(1)}, bf16[8,48,256]{2,1,0:T(8,128)(2,1)}, u32[]{:S(2)}, u32[]{:S(2)}) collective-permute-start(bf16[8,48,256]{2,1,0:T(8,128)(2,1)S(1)} %fusion.47), channel_id=1, source_target_pairs={{0,8},{8,16},{16,24},{1,9},{9,17},{17,25},{2,10},{10,18},{18,26},{... | collective-permute-start | bytes 589832 | tf_op jit(solution)/shard_map/ppermute | solution.py:21
  48.2 5.8 %all-to-all-start = ((bf16[8,1,48,512]{3,2,1,0:T(8,128)(2,1)}), bf16[8,1,48,512]{3,2,1,0:T(8,128)(2,1)S(1)}, u32[]{:S(2)}, u32[]{:S(2)}) async-start(bf16[8,1,48,512]{3,2,1,0:T(8,128)(2,1)} %fusion.130), calls=%async_computation | async-start | bytes 786432 | tf_op jit(solution)/shard_map/all_to_all | solution.py:151
  54.1 9.2 %all-to-all-done = bf16[8,1,48,512]{3,2,1,0:T(8,128)(2,1)S(1)} async-done(((bf16[8,1,48,512]{3,2,1,0:T(8,128)(2,1)}), bf16[8,1,48,512]{3,2,1,0:T(8,128)(2,1)S(1)}, u32[]{:S(2)}, u32[]{:S(2)}) %all-to-all-start) | async-done | bytes 393248 | tf_op jit(solution)/shard_map/all_to_all | solution.py:151
  64.1 3.2 %convolution_convert_fusion.1 = bf16[384,1536]{1,0:T(8,128)(2,1)} fusion(bf16[384,512]{1,0:T(8,128)(2,1)S(1)} %fusion.39, bf16[512,1536]{1,0:T(8,128)(2,1)} %param.25), kind=kOutput, calls=%fused_computation.25 | convolution fusion | flops 604569600 | bytes 3145728 | tf_op jit(solution)/shard_map/while/body/eval_jaxpr/dot_general | solution.py:75
  67.3 2.4 %copy.148 = bf16[384,1536]{0,1:T(8,128)(2,1)} copy(bf16[384,1536]{1,0:T(8,128)(2,1)} %convolution_convert_fusion.1) | data formatting | bytes 2359296 | tf_op jit(solution)/shard_map/while/body/eval_jaxpr/convert_element_type | solution.py:75
  69.7 2.1 %slice_bitcast_fusion = (bf16[8,384,64]{1,2,0:T(8,128)(2,1)}, bf16[8,384,64]{1,2,0:T(8,128)(2,1)S(1)}, bf16[8,384,64]{1,2,0:T(8,128)(2,1)S(1)}) fusion(bf16[384,3,8,64]{0,3,2,1:T(8,128)(2,1)} %bitcast.175), kind=kLoop, calls=%fused_computation.70 | loop fusion | bytes 2359296 | tf_op jit(solution)/shard_map/while/body/eval_jaxpr/transpose | solution.py:64
  71.8 16.7 %while.17 = (s32[]{:T(128)}, bf16[8,384,64]{1,2,0:T(8,128)(2,1)}, pred[384]{0:T(512)(128)(4,1)S(1)}, bf16[8,384,64]{1,2,0:T(8,128)(2,1)S(1)}, bf16[8,384,64]{1,2...) while((s32[]{:T(128)}, bf16[8,384,64]{1,2,0:T(8,128)(2,1)}, pred[384]{0:T(512)(128)(4,1)S(1)}, ...), condition=%wide.region_7.8_spmd, body=%wide.region_4.7_spmd.sunk | while | flops 38952192 | bytes 1976397 | solution.py:59
  72.2 1.7 %fusion.194 = bf16[8,384,64]{1,2,0:T(8,128)(2,1)} fusion(bf16[8,384,64]{1,2,0:T(8,128)(2,1)} %get-tuple-element.228, s32[]{:T(128)} %get-tuple-element.227, f32[384,384]{0,1:T(8,128)S(1)} %get-tuple-element.218, f32[384]{0:T(512)S(1)} %fusion.193, f32[384]{0:T(512)S(1)} %get-tuple-element.219, bf16[8,384,64]{1,2,0:T(8,128)(2,1)} %get-tuple-element.239), kind=kOutput, calls=%fused_computation.4.clone.1 | convolution fusion | flops 19341312 | bytes 692224 | tf_op jit(solution)/shard_map/while/body/eval_jaxpr/while/body/eval_jaxpr/while/body/eval_jaxpr/dot_general | solution.py:53
  74.3 1.7 %fusion.194 = bf16[8,384,64]{1,2,0:T(8,128)(2,1)} fusion(bf16[8,384,64]{1,2,0:T(8,128)(2,1)} %get-tuple-element.228, s32[]{:T(128)} %get-tuple-element.227, f32[384,384]{0,1:T(8,128)S(1)} %get-tuple-element.218, f32[384]{0:T(512)S(1)} %fusion.193, f32[384]{0:T(512)S(1)} %get-tuple-element.219, bf16[8,384,64]{1,2,0:T(8,128)(2,1)} %get-tuple-element.239), kind=kOutput, calls=%fused_computation.4.clone.1 | convolution fusion | flops 19341312 | bytes 692224 | tf_op jit(solution)/shard_map/while/body/eval_jaxpr/while/body/eval_jaxpr/while/body/eval_jaxpr/dot_general | solution.py:53
  76.4 1.7 %fusion.194 = bf16[8,384,64]{1,2,0:T(8,128)(2,1)} fusion(bf16[8,384,64]{1,2,0:T(8,128)(2,1)} %get-tuple-element.228, s32[]{:T(128)} %get-tuple-element.227, f32[384,384]{0,1:T(8,128)S(1)} %get-tuple-element.218, f32[384]{0:T(512)S(1)} %fusion.193, f32[384]{0:T(512)S(1)} %get-tuple-element.219, bf16[8,384,64]{1,2,0:T(8,128)(2,1)} %get-tuple-element.239), kind=kOutput, calls=%fused_computation.4.clone.1 | convolution fusion | flops 19341312 | bytes 692224 | tf_op jit(solution)/shard_map/while/body/eval_jaxpr/while/body/eval_jaxpr/while/body/eval_jaxpr/dot_general | solution.py:53
  78.5 1.7 %fusion.194 = bf16[8,384,64]{1,2,0:T(8,128)(2,1)} fusion(bf16[8,384,64]{1,2,0:T(8,128)(2,1)} %get-tuple-element.228, s32[]{:T(128)} %get-tuple-element.227, f32[384,384]{0,1:T(8,128)S(1)} %get-tuple-element.218, f32[384]{0:T(512)S(1)} %fusion.193, f32[384]{0:T(512)S(1)} %get-tuple-element.219, bf16[8,384,64]{1,2,0:T(8,128)(2,1)} %get-tuple-element.239), kind=kOutput, calls=%fused_computation.4.clone.1 | convolution fusion | flops 19341312 | bytes 692224 | tf_op jit(solution)/shard_map/while/body/eval_jaxpr/while/body/eval_jaxpr/while/body/eval_jaxpr/dot_general | solution.py:53
  80.6 1.7 %fusion.194 = bf16[8,384,64]{1,2,0:T(8,128)(2,1)} fusion(bf16[8,384,64]{1,2,0:T(8,128)(2,1)} %get-tuple-element.228, s32[]{:T(128)} %get-tuple-element.227, f32[384,384]{0,1:T(8,128)S(1)} %get-tuple-element.218, f32[384]{0:T(512)S(1)} %fusion.193, f32[384]{0:T(512)S(1)} %get-tuple-element.219, bf16[8,384,64]{1,2,0:T(8,128)(2,1)} %get-tuple-element.239), kind=kOutput, calls=%fused_computation.4.clone.1 | convolution fusion | flops 19341312 | bytes 692224 | tf_op jit(solution)/shard_map/while/body/eval_jaxpr/while/body/eval_jaxpr/while/body/eval_jaxpr/dot_general | solution.py:53
  82.7 1.7 %fusion.194 = bf16[8,384,64]{1,2,0:T(8,128)(2,1)} fusion(bf16[8,384,64]{1,2,0:T(8,128)(2,1)} %get-tuple-element.228, s32[]{:T(128)} %get-tuple-element.227, f32[384,384]{0,1:T(8,128)S(1)} %get-tuple-element.218, f32[384]{0:T(512)S(1)} %fusion.193, f32[384]{0:T(512)S(1)} %get-tuple-element.219, bf16[8,384,64]{1,2,0:T(8,128)(2,1)} %get-tuple-element.239), kind=kOutput, calls=%fused_computation.4.clone.1 | convolution fusion | flops 19341312 | bytes 692224 | tf_op jit(solution)/shard_map/while/body/eval_jaxpr/while/body/eval_jaxpr/while/body/eval_jaxpr/dot_general | solution.py:53
  84.8 1.7 %fusion.194 = bf16[8,384,64]{1,2,0:T(8,128)(2,1)} fusion(bf16[8,384,64]{1,2,0:T(8,128)(2,1)} %get-tuple-element.228, s32[]{:T(128)} %get-tuple-element.227, f32[384,384]{0,1:T(8,128)S(1)} %get-tuple-element.218, f32[384]{0:T(512)S(1)} %fusion.193, f32[384]{0:T(512)S(1)} %get-tuple-element.219, bf16[8,384,64]{1,2,0:T(8,128)(2,1)} %get-tuple-element.239), kind=kOutput, calls=%fused_computation.4.clone.1 | convolution fusion | flops 19341312 | bytes 692224 | tf_op jit(solution)/shard_map/while/body/eval_jaxpr/while/body/eval_jaxpr/while/body/eval_jaxpr/dot_general | solution.py:53
  86.9 1.7 %fusion.194 = bf16[8,384,64]{1,2,0:T(8,128)(2,1)} fusion(bf16[8,384,64]{1,2,0:T(8,128)(2,1)} %get-tuple-element.228, s32[]{:T(128)} %get-tuple-element.227, f32[384,384]{0,1:T(8,128)S(1)} %get-tuple-element.218, f32[384]{0:T(512)S(1)} %fusion.193, f32[384]{0:T(512)S(1)} %get-tuple-element.219, bf16[8,384,64]{1,2,0:T(8,128)(2,1)} %get-tuple-element.239), kind=kOutput, calls=%fused_computation.4.clone.1 | convolution fusion | flops 19341312 | bytes 692224 | tf_op jit(solution)/shard_map/while/body/eval_jaxpr/while/body/eval_jaxpr/while/body/eval_jaxpr/dot_general | solution.py:53
  88.5 1.7 %fusion.173 = (f32[384]{0:T(512)S(1)}, f32[384,512]{1,0:T(8,128)S(1)}) fusion(bf16[384,512]{0,1:T(8,128)(2,1)} %bitcast.178, bf16[512,512]{1,0:T(8,128)(2,1)} %param.26, bf16[384,512]{1,0:T(8,128)(2,1)S(1)} %bitcast.174), kind=kOutput, calls=%fused_computation.204 | convolution fusion | flops 202309248 | bytes 2098688 | tf_op jit(solution)/shard_map/while/body/eval_jaxpr/dot_general | solution.py:80
  90.5 4.4 %fusion.30 = bf16[1,384,512]{2,1,0:T(8,128)(2,1)} fusion(f32[384,512]{1,0:T(8,128)S(1)} %get-tuple-element.178, bf16[2048,512]{1,0:T(8,128)(2,1)S(1)} %copy-done, bf16[512,2048]{1,0:T(8,128)(2,1)} %param.28, f32[512]{0:T(512)S(1)} %copy-done.6, f32[384]{0:T(512)S(1)} %add_rsqrt_fusion.1, f32[384]{0:T(512)S(1)} %broadcast_multiply_fusion.1), kind=kOutput, calls=%fused_computation.33 | convolution fusion | flops 1618870272 | bytes 5379072 | tf_op jit(solution)/shard_map/while/body/eval_jaxpr/dot_general | solution.py:87
  97.0 3.0 %reduce.4 = bf16[384,512]{1,0:T(8,128)(2,1)S(1)} reduce(bf16[384,1,512]{2,1,0:T(2,128)(2,1)S(1)} %bitcast.176, bf16[]{:T(256)} %broadcast.174), dimensions={1}, to_apply=%bitcast.165.reduce_sub_computation | reduce | bytes 786434
  100.3 19.2 %all_to_all.17 = bf16[8,2,12288]{2,1,0:T(2,128)(2,1)S(1)} all-to-all(bf16[8,2,12288]{2,1,0:T(2,128)(2,1)S(1)} %reshape.97), channel_id=1, replica_groups=mesh['tm'=4,'chan'=8] {'chan'}, dimensions={0} | all-to-all | bytes 786432 | tf_op jit(solution)/shard_map/all_to_all | solution.py:170
  (111 shorter events, 30.6 us)
Async XLA Ops:
  0.0 90.4 %copy-start = (bf16[2048,512]{1,0:T(8,128)(2,1)S(1)}, bf16[2048,512]{1,0:T(8,128)(2,1)}, u32[]{:S(2)}) copy-start(bf16[2048,512]{1,0:T(8,128)(2,1)} %param.29) | copy-start | bytes 6291460
  0.0 25.9 %copy-start.3 = (bf16[3,64,128]{2,1,0:T(8,128)(2,1)S(1)}, bf16[3,64,128]{2,1,0:T(8,128)(2,1)}, u32[]{:S(2)}) copy-start(bf16[3,64,128]{2,1,0:T(8,128)(2,1)} %param.20) | copy-start | bytes 147460
  0.0 28.4 %copy-start.2 = (bf16[3,128,256]{2,1,0:T(8,128)(2,1)S(1)}, bf16[3,128,256]{2,1,0:T(8,128)(2,1)}, u32[]{:S(2)}) copy-start(bf16[3,128,256]{2,1,0:T(8,128)(2,1)} %param.21) | copy-start | bytes 589828
  1.6 3.8 %collective-permute-start = (bf16[48,2]{0,1:T(2,128)(2,1)S(1)}, bf16[48,2]{0,1:T(2,128)(2,1)S(1)}, u32[]{:S(2)}, u32[]{:S(2)}) collective-permute-start(bf16[48,2]{0,1:T(2,128)(2,1)S(1)} %get-tuple-element.175), channel_id=1, source_target_pairs={{0,8},{8,16},{16,24},{1,9},{9,17},{17,25},{2,10},{10,18},{18,26},{... | collective-permute-start | bytes 584 | tf_op jit(solution)/shard_map/ppermute | solution.py:21
  4.0 5.1 %collective-permute-start.1 = (bf16[48,2]{0,1:T(2,128)(2,1)S(1)}, bf16[48,2]{0,1:T(2,128)(2,1)S(1)}, u32[]{:S(2)}, u32[]{:S(2)}) collective-permute-start(bf16[48,2]{0,1:T(2,128)(2,1)S(1)} %get-tuple-element.176), channel_id=1, source_target_pairs={{8,0},{16,8},{24,16},{9,1},{17,9},{25,17},{10,2},{18,10},{26,18},{... | collective-permute-start | bytes 584 | tf_op jit(solution)/shard_map/ppermute | solution.py:23
  10.3 7.1 %collective-permute-start.3 = (bf16[1,48,32]{1,2,0:T(8,128)(2,1)S(1)}, bf16[1,48,32]{1,2,0:T(8,128)(2,1)S(1)}, u32[]{:S(2)}, u32[]{:S(2)}) collective-permute-start(bf16[1,48,32]{1,2,0:T(8,128)(2,1)S(1)} %get-tuple-element.174), channel_id=1, source_target_pairs={{8,0},{16,8},{24,16},{9,1},{17,9},{25,17},{10,2},{18,10},{26,18},{... | collective-permute-start | bytes 9224 | tf_op jit(solution)/shard_map/ppermute | solution.py:23
  11.6 6.7 %collective-permute-start.2 = (bf16[1,48,32]{1,2,0:T(8,128)(2,1)S(1)}, bf16[1,48,32]{1,2,0:T(8,128)(2,1)S(1)}, u32[]{:S(2)}, u32[]{:S(2)}) collective-permute-start(bf16[1,48,32]{1,2,0:T(8,128)(2,1)S(1)} %get-tuple-element.173), channel_id=1, source_target_pairs={{0,8},{8,16},{16,24},{1,9},{9,17},{17,25},{2,10},{10,18},{18,26},{... | collective-permute-start | bytes 9224 | tf_op jit(solution)/shard_map/ppermute | solution.py:21
  19.3 22.0 %copy-start.1 = (bf16[3,256,256]{2,1,0:T(8,128)(2,1)S(1)}, bf16[3,256,256]{2,1,0:T(8,128)(2,1)}, u32[]{:S(2)}) copy-start(bf16[3,256,256]{2,1,0:T(8,128)(2,1)} %param.22) | copy-start | bytes 1179652
  19.3 6.6 %collective-permute-start.5 = (bf16[2,48,64]{2,1,0:T(8,128)(2,1)S(1)}, bf16[2,48,64]{2,1,0:T(8,128)(2,1)S(1)}, u32[]{:S(2)}, u32[]{:S(2)}) collective-permute-start(bf16[2,48,64]{2,1,0:T(8,128)(2,1)S(1)} %get-tuple-element.172), channel_id=1, source_target_pairs={{8,0},{16,8},{24,16},{9,1},{17,9},{25,17},{10,2},{18,10},{26,18},{... | collective-permute-start | bytes 36872 | tf_op jit(solution)/shard_map/ppermute | solution.py:23
  21.6 5.1 %collective-permute-start.4 = (bf16[2,48,64]{2,1,0:T(8,128)(2,1)S(1)}, bf16[2,48,64]{2,1,0:T(8,128)(2,1)S(1)}, u32[]{:S(2)}, u32[]{:S(2)}) collective-permute-start(bf16[2,48,64]{2,1,0:T(8,128)(2,1)S(1)} %get-tuple-element.171), channel_id=1, source_target_pairs={{0,8},{8,16},{16,24},{1,9},{9,17},{17,25},{2,10},{10,18},{18,26},{... | collective-permute-start | bytes 36872 | tf_op jit(solution)/shard_map/ppermute | solution.py:21
  26.9 14.8 %copy-start.5 = (bf16[256,512]{1,0:T(8,128)(2,1)S(1)}, bf16[256,512]{1,0:T(8,128)(2,1)}, u32[]{:S(2)}) copy-start(bf16[256,512]{1,0:T(8,128)(2,1)} %param.23) | copy-start | bytes 786436
  27.0 6.0 %collective-permute-start.7 = (bf16[4,48,128]{2,1,0:T(8,128)(2,1)S(1)}, bf16[4,48,128]{2,1,0:T(8,128)(2,1)S(1)}, u32[]{:S(2)}, u32[]{:S(2)}) collective-permute-start(bf16[4,48,128]{2,1,0:T(8,128)(2,1)S(1)} %get-tuple-element.170), channel_id=1, source_target_pairs={{8,0},{16,8},{24,16},{9,1},{17,9},{25,17},{10,2},{18,10},{26,18},{... | collective-permute-start | bytes 147464 | tf_op jit(solution)/shard_map/ppermute | solution.py:23
  28.6 5.2 %collective-permute-start.6 = (bf16[4,48,128]{2,1,0:T(8,128)(2,1)S(1)}, bf16[4,48,128]{2,1,0:T(8,128)(2,1)S(1)}, u32[]{:S(2)}, u32[]{:S(2)}) collective-permute-start(bf16[4,48,128]{2,1,0:T(8,128)(2,1)S(1)} %get-tuple-element.169), channel_id=1, source_target_pairs={{0,8},{8,16},{16,24},{1,9},{9,17},{17,25},{2,10},{10,18},{18,26},{... | collective-permute-start | bytes 147464 | tf_op jit(solution)/shard_map/ppermute | solution.py:21
  34.1 7.3 %collective-permute-start.9 = (bf16[8,48,256]{2,1,0:T(8,128)(2,1)S(1)}, bf16[8,48,256]{2,1,0:T(8,128)(2,1)S(1)}, u32[]{:S(2)}, u32[]{:S(2)}) collective-permute-start(bf16[8,48,256]{2,1,0:T(8,128)(2,1)S(1)} %fusion.47), channel_id=1, source_target_pairs={{8,0},{16,8},{24,16},{9,1},{17,9},{25,17},{10,2},{18,10},{26,18},{... | collective-permute-start | bytes 589832 | tf_op jit(solution)/shard_map/ppermute | solution.py:23
  35.4 6.3 %collective-permute-start.8 = (bf16[8,48,256]{2,1,0:T(8,128)(2,1)S(1)}, bf16[8,48,256]{2,1,0:T(8,128)(2,1)}, u32[]{:S(2)}, u32[]{:S(2)}) collective-permute-start(bf16[8,48,256]{2,1,0:T(8,128)(2,1)S(1)} %fusion.47), channel_id=1, source_target_pairs={{0,8},{8,16},{16,24},{1,9},{9,17},{17,25},{2,10},{10,18},{18,26},{... | collective-permute-start | bytes 589832 | tf_op jit(solution)/shard_map/ppermute | solution.py:21
  41.5 12.5 %copy-start.7 = (s32[12]{0:T(128)S(1)}, s32[12]{0:T(128)}, u32[]{:S(2)}) copy-start(s32[12]{0:T(128)} %param.17) | copy-start | bytes 148
  41.7 22.2 %copy-start.4 = (f32[512]{0:T(512)S(1)}, f32[512]{0:T(512)}, u32[]{:S(2)}) copy-start(f32[512]{0:T(512)} %param.24) | copy-start | bytes 6148
  48.2 15.1 %all-to-all-start = ((bf16[8,1,48,512]{3,2,1,0:T(8,128)(2,1)}), bf16[8,1,48,512]{3,2,1,0:T(8,128)(2,1)S(1)}, u32[]{:S(2)}, u32[]{:S(2)}) async-start(bf16[8,1,48,512]{3,2,1,0:T(8,128)(2,1)} %fusion.130), calls=%async_computation | async-start | bytes 786432 | tf_op jit(solution)/shard_map/all_to_all | solution.py:151
  88.5 1.9 %copy-start.6 = (f32[512]{0:T(512)S(1)}, f32[512]{0:T(512)}, u32[]{:S(2)}) copy-start(f32[512]{0:T(512)} %param.27) | copy-start | bytes 6148
